TPU v7x, 128 devices: a whole 4x4x4 slice. The times are simulated.
128 devices in a mesh: seq: 16 (over y, z_lo, core), tp: 8 (over z_hi, x).
Axes of the slice: x: 4, y: 4, z: 4 (z_hi: 2, z_lo: 2; z = z_hi * 2 + z_lo), core: 2. Of those that a mesh axis runs over, the one named last changes fastest.
Arguments:
- tokens: bfloat16 [8192, 2048], P('seq'), may hold values from -6 to 6
- w_zx: float32 [2048, 8192], P(('seq', 'tp')), may hold values from -0.125 to 0.125
- w_dt: float32 [2048, 64], P(('seq', 'tp')), may hold values from -0.26516503 to 0.26516503
- w_bc: float32 [2048, 256], P(('seq', 'tp')), may hold values from -0.125 to 0.125
- conv_x_weight: float32 [4, 4096], P(None, 'tp'), may hold values from -3 to 3
- conv_x_bias: float32 [4096], P('tp'), may hold values from -1.8 to 1.8
- conv_bc_weight: float32 [4, 256], replicated, may hold values from -3 to 3
- conv_bc_bias: float32 [256], replicated, may hold values from -1.8 to 1.8
- dt_bias: float32 [64], P('tp'), may hold values from -11 to -2
- a_log: float32 [64], P('tp'), may hold values from 0 to 2.77
- skip: float32 [64], P('tp'), may hold values from 0.5 to 2
- norm_weight: float32 [4096], P('tp'), may hold values from 0.1 to 1.9
- w_out: float32 [4096, 2048], P('tp', 'seq'), may hold values from -0.09375 to 0.09375
- lengths: int32 [8], replicated, may hold values from 1 to 4096, 8192 in all
- request_group: int32 [32], replicated, may hold values from 0 to 31
Outputs:
- mixed: bfloat16 [8192, 2048], P(('seq', 'tp'))
- request_states: float32 [32, 64, 64, 128], P('seq', 'tp')
Inputs may be any that keep to these rules, and one draw needn't show every extreme that they name: 8 prompts packed end to end in this order; the lengths sum to 8192 and the longest is exactly 4096.
All inputs are finite; a program needn't handle non-finite values.
Results may differ from a plain program's by a relative error of at most 0.011.
Values may be sent and summed in bfloat16 or wider, within the bound.
A program may use at most 128 MiB of HBM per device.

v0:
```python
import jax
import jax.numpy as jnp
from jax import lax
from jax.sharding import PartitionSpec as P

INNER = 4096
GROUP = 256
epsilon = 1e-05


def from_behind(x, axis, by):
    count = lax.axis_size(axis)
    pairs = [(i, i + by) for i in range(count) if 0 <= i + by < count]
    return lax.ppermute(x, axis, pairs)


def segment_of(position, lengths):
    prompt_ends = jnp.cumsum(lengths)
    return jnp.sum((position[:, None] >= prompt_ends[None, :]).astype(jnp.int32), axis=1)


def round_up(n, m):
    return (n + m - 1) // m * m


def on_device(
    tokens,
    w_zx,
    w_dt,
    w_bc,
    conv_x_weight,
    conv_x_bias,
    conv_bc_weight,
    conv_bc_bias,
    dt_bias,
    a_log,
    skip,
    norm_weight,
    w_out,
    lengths,
    request_group,
):
    tp_count = lax.axis_size("tp")
    seq_count = lax.axis_size("seq")
    seq_index = lax.axis_index("seq")
    tok_dev = tokens.shape[0]
    local_rows = w_zx.shape[0]
    inner_local = conv_x_weight.shape[1]
    heads_local = dt_bias.shape[0]
    head_width = inner_local // heads_local
    bc_width = conv_bc_weight.shape[1]
    state_width = bc_width // 2
    taps = conv_x_weight.shape[0]
    groups_dev = tok_dev // GROUP
    zx_part = w_zx.astype(jnp.bfloat16).reshape(local_rows, 2, tp_count, inner_local)
    zx_part = zx_part.transpose(0, 2, 1, 3).reshape(local_rows, tp_count, 2 * inner_local)
    bc_part = jnp.broadcast_to(
        w_bc.astype(jnp.bfloat16)[:, None, :], (local_rows, tp_count, bc_width)
    )
    dt_part = w_dt.astype(jnp.bfloat16).reshape(local_rows, tp_count, heads_local)
    used = 2 * inner_local + bc_width + heads_local
    width = round_up(used, 128)
    pad_part = jnp.zeros((local_rows, tp_count, width - used), jnp.bfloat16)
    packed = jnp.concatenate([zx_part, bc_part, dt_part, pad_part], axis=2)
    packed = packed.reshape(local_rows, tp_count * width)
    block = lax.all_to_all(packed, "tp", split_axis=1, concat_axis=0, tiled=True)
    out_rows, out_cols = w_out.shape
    block_rows = block.shape[0]
    out_piece = w_out.astype(jnp.bfloat16).reshape(block_rows, out_rows * out_cols // block_rows)
    gathered = lax.all_gather(
        jnp.concatenate([block, out_piece], axis=1), "seq", axis=0, tiled=True
    )
    weights = gathered[:, :width]
    out_block = gathered[:, width:].reshape(seq_count, out_rows, out_cols)
    out_block = out_block.transpose(1, 0, 2).reshape(out_rows, seq_count * out_cols)
    proj = jnp.dot(tokens, weights, preferred_element_type=jnp.float32)
    zx_low = proj[:, : 2 * inner_local].astype(jnp.bfloat16)
    gate_z = zx_low[:, :inner_local]
    x_raw = zx_low[:, inner_local:]
    bc_raw = proj[:, 2 * inner_local : 2 * inner_local + bc_width].astype(jnp.bfloat16)
    dt_pre = proj[:, 2 * inner_local + bc_width : used]
    raw_mix = jnp.concatenate([x_raw, bc_raw], axis=1)
    conv_weight = jnp.concatenate([conv_x_weight, conv_bc_weight], axis=1)
    conv_bias = jnp.concatenate([conv_x_bias, conv_bc_bias], axis=0)
    rim_rows = from_behind(raw_mix[tok_dev - (taps - 1) :], "seq", 1)
    padded = jnp.concatenate([rim_rows, raw_mix], axis=0)
    offset = seq_index * tok_dev
    seg_pad = segment_of(
        offset - (taps - 1) + jnp.arange(tok_dev + taps - 1, dtype=jnp.int32), lengths
    )
    seg_tok = seg_pad[taps - 1 :]
    conv_sum = jnp.zeros((tok_dev, raw_mix.shape[1]), jnp.float32) + conv_bias[None, :]
    for offset_tap in range(taps):
        rows_wide = padded[offset_tap : offset_tap + tok_dev].astype(jnp.float32)
        keep_tap = seg_pad[offset_tap : offset_tap + tok_dev] == seg_tok
        conv_sum = conv_sum + jnp.where(
            keep_tap[:, None], rows_wide * conv_weight[offset_tap][None, :], 0.0
        )
    convolved = jax.nn.silu(conv_sum).astype(jnp.bfloat16)
    inputs = convolved[:, :inner_local].reshape(groups_dev, GROUP, heads_local, head_width)
    b_matrix = convolved[:, inner_local : inner_local + state_width].reshape(
        groups_dev, GROUP, state_width
    )
    c_matrix = convolved[:, inner_local + state_width :].reshape(groups_dev, GROUP, state_width)
    step_size = jax.nn.softplus(dt_pre + dt_bias[None, :]).reshape(groups_dev, GROUP, heads_local)
    step_heads = step_size.transpose(0, 2, 1)
    decay_rate = -jnp.exp(a_log)
    cumul_heads = jnp.cumsum(step_size * decay_rate[None, None, :], axis=1).transpose(0, 2, 1)
    segments = seg_tok.reshape(groups_dev, GROUP)
    seg_before = segment_of(offset + jnp.arange(groups_dev, dtype=jnp.int32) * GROUP - 1, lengths)
    within = jnp.arange(GROUP, dtype=jnp.int32)
    same_prompt = (segments[:, :, None] == segments[:, None, :]) & (
        within[:, None] >= within[None, :]
    )[None]
    log_decay = cumul_heads[:, :, :, None] - cumul_heads[:, :, None, :]
    decay_matrix = jnp.where(
        same_prompt[:, None], jnp.exp(jnp.where(same_prompt[:, None], log_decay, 0.0)), 0.0
    )
    scores = jnp.einsum("cin,cjn->cij", c_matrix, b_matrix, preferred_element_type=jnp.float32)
    mix_weights = (decay_matrix * scores[:, None] * step_heads[:, :, None, :]).astype(jnp.bfloat16)
    diag_out = jnp.einsum(
        "chij,cjhp->cihp", mix_weights, inputs, preferred_element_type=jnp.float32
    )
    last_segment = segments[:, -1]
    tail_weight = (
        jnp.where(
            (segments == last_segment[:, None])[:, None, :],
            jnp.exp(cumul_heads[:, :, -1:] - cumul_heads),
            0.0,
        )
        * step_heads
    )
    b_weighted = (b_matrix.astype(jnp.float32)[:, None] * tail_weight[:, :, :, None]).astype(
        jnp.bfloat16
    )
    contrib = jnp.einsum("cjhp,chjn->chpn", inputs, b_weighted, preferred_element_type=jnp.float32)
    pass_gate = jnp.where(
        (last_segment == seg_before)[:, None], jnp.exp(cumul_heads[:, :, -1]), 0.0
    )

    def local_step(carry_state, group_item):
        factor, source = group_item
        next_state = factor[:, None, None] * carry_state + source
        return (next_state, (carry_state, next_state))

    zero_state = jnp.zeros((heads_local, head_width, state_width), jnp.float32)
    _, (local_in, local_end) = lax.scan(local_step, zero_state, (pass_gate, contrib))
    through_group = jnp.cumprod(pass_gate, axis=0)
    before_group = jnp.concatenate(
        [jnp.ones((1, heads_local), jnp.float32), through_group[:-1]], axis=0
    )
    gate_hi = through_group.astype(jnp.bfloat16)
    gate_lo = (through_group - gate_hi.astype(jnp.float32)).astype(jnp.bfloat16)
    extra = jnp.zeros((groups_dev, heads_local, 8, state_width), jnp.bfloat16)
    extra = extra.at[:, :, 0, :].set(
        jnp.broadcast_to(gate_hi[:, :, None], gate_hi.shape + (state_width,))
    )
    extra = extra.at[:, :, 1, :].set(
        jnp.broadcast_to(gate_lo[:, :, None], gate_lo.shape + (state_width,))
    )
    sendable = jnp.concatenate([local_end.astype(jnp.bfloat16), extra], axis=2)
    every = lax.all_gather(sendable, "seq", axis=0, tiled=False)
    every_end = every[:, :, :, :head_width].astype(jnp.float32)
    every_gate = every[:, :, :, head_width, 0].astype(jnp.float32) + every[
        :, :, :, head_width + 1, 0
    ].astype(jnp.float32)
    dev_gate = every_gate[:, -1]
    dev_ids = jnp.arange(seq_count, dtype=jnp.int32)

    def carry_weights(k):
        between = (dev_ids[:, None] < dev_ids[None, :]) & (dev_ids[None, :] < k)
        factors = jnp.where(between[:, :, None], dev_gate[None, :, :], 1.0)
        return jnp.where((dev_ids < k)[:, None], jnp.prod(factors, axis=1), 0.0)

    own_weights = carry_weights(seq_index)
    slot_ids = jnp.arange(groups_dev, dtype=jnp.int32)
    last_slot = (slot_ids == groups_dev - 1).astype(jnp.float32)
    own_coef = own_weights[:, None, :] * last_slot[None, :, None]
    carried = jnp.einsum(
        "jch,jchpn->hpn",
        own_coef,
        every_end,
        precision=lax.Precision.HIGHEST,
        preferred_element_type=jnp.float32,
    )
    group_in = before_group[:, :, None, None] * carried[None] + local_in
    state_low = group_in.astype(jnp.bfloat16)
    carry_keep = jnp.where((segments == seg_before[:, None])[:, None, :], jnp.exp(cumul_heads), 0.0)
    carry_out = jnp.einsum(
        "cin,chpn->cihp", c_matrix, state_low, preferred_element_type=jnp.float32
    )
    carry_out = carry_out * carry_keep.transpose(0, 2, 1)[:, :, :, None]
    y_local = diag_out + carry_out + skip[None, None, :, None] * inputs.astype(jnp.float32)
    y_local = y_local.reshape(tok_dev, inner_local)
    gated = y_local * jax.nn.silu(gate_z.astype(jnp.float32))
    square_sum = jnp.sum(gated * gated, axis=1)
    scaled = (gated * norm_weight[None, :]).astype(jnp.bfloat16)
    partial = jnp.dot(scaled, out_block, preferred_element_type=jnp.float32)
    side = jnp.zeros((tok_dev, 128), jnp.float32).at[:, 0].set(square_sum)
    summed = lax.psum_scatter(
        jnp.concatenate([partial, side], axis=1).astype(jnp.bfloat16),
        "tp",
        scatter_dimension=0,
        tiled=True,
    ).astype(jnp.float32)
    d_model = out_block.shape[1]
    mean_square = summed[:, d_model] / INNER
    mixed = (summed[:, :d_model] * lax.rsqrt(mean_square + epsilon)[:, None]).astype(jnp.bfloat16)
    req_dev = request_group.shape[0] // seq_count
    mine = lax.dynamic_slice_in_dim(request_group, seq_index * req_dev, req_dev)
    req_k = mine // groups_dev
    req_c = mine % groups_dev
    req_w = jax.vmap(carry_weights)(req_k)
    req_gate = every_gate[req_k, req_c]
    coef = req_gate[:, None, None, :] * req_w[:, :, None, :] * last_slot[None, None, :, None]
    hit = (dev_ids[None, :, None] == req_k[:, None, None]) & (
        slot_ids[None, None, :] == req_c[:, None, None]
    )
    coef = coef + hit[:, :, :, None].astype(jnp.float32)
    request_states = jnp.einsum(
        "rjch,jchpn->rhpn",
        coef,
        every_end,
        precision=lax.Precision.HIGHEST,
        preferred_element_type=jnp.float32,
    )
    return (mixed.astype(jnp.bfloat16), request_states)


def solution(mesh):
    return jax.shard_map(
        on_device,
        mesh=mesh,
        in_specs=(
            P("seq", None),
            P(("seq", "tp"), None),
            P(("seq", "tp"), None),
            P(("seq", "tp"), None),
            P(None, "tp"),
            P("tp"),
            P(),
            P(),
            P("tp"),
            P("tp"),
            P("tp"),
            P("tp"),
            P("tp", "seq"),
            P(),
            P(),
        ),
        out_specs=(P(("seq", "tp"), None), P("seq", "tp", None, None)),
        check_vma=False,
    )
```

profile of v0, /device:TPU:0, one launch (start us, length us, event | category | flops | bytes accessed | tf_op | source)
XLA Modules:
  0.0 252.9 jit_solution(9752416855945971542)
XLA Ops:
  11.4 7.7 %all-to-all-start = ((bf16[16,8,1408]{2,0,1:T(8,128)(2,1)}), bf16[16,8,1408]{2,0,1:T(8,128)(2,1)S(1)}, u32[]{:S(2)}, u32[]{:S(2)}) async-start(bf16[16,8,1408]{2,0,1:T(8,128)(2,1)} %concatenate.38), calls=%async_computation | async-start | bytes 720896 | tf_op jit(solution)/shard_map/all_to_all | solution.py:66
  19.3 9.7 %all-to-all-done = bf16[16,8,1408]{2,0,1:T(8,128)(2,1)S(1)} async-done(((bf16[16,8,1408]{2,0,1:T(8,128)(2,1)}), bf16[16,8,1408]{2,0,1:T(8,128)(2,1)S(1)}, u32[]{:S(2)}, u32[]{:S(2)}) %all-to-all-start) | async-done | bytes 360480 | tf_op jit(solution)/shard_map/all_to_all | solution.py:66
  32.9 44.3 %all-gather.4.cloned.1.call-done = bf16[2048,1920]{1,0:T(8,128)(2,1)} async-done(((bf16[128,1920]{1,0:T(8,128)(2,1)}), bf16[2048,1920]{1,0:T(8,128)(2,1)}) %all-gather.4.cloned.1.call-update) | async-done | bytes 7864336 | tf_op jit(solution)/shard_map/all_gather | solution.py:70
  77.2 7.0 %fusion.65 = (bf16[512,1408]{0,1:T(8,128)(2,1)}, f32[512,1408]{0,1:T(8,128)S(1)}) fusion(bf16[512,2048]{1,0:T(8,128)(2,1)S(1)} %copy-done, bf16[2048,1920]{1,0:T(8,128)(2,1)} %all-gather.4.cloned.1.call-done), kind=kOutput, calls=%fused_computation.143 | convolution fusion | flops 2953510912 | bytes 12189696 | tf_op jit(solution)/shard_map/dot_general | solution.py:76
  87.6 2.2 collective-permute-start
  90.6 1.2 slice.204
  93.2 1.4 scatter.11
  94.5 2.9 %multiply_convert_fusion.3 = bf16[512,768]{0,1:T(8,128)(2,1)S(1)} fusion(bf16[512,768]{0,1:T(8,128)(2,1)S(1)} %slice.204, bf16[3,768]{0,1:T(8,128)(2,1)S(1)} %collective-permute-done, f32[768]{0:T(1024)} %get-tuple-element.107, f32[768]{0:T(1024)} %get-tuple-element.108, f32[768]{0:T(1024)} %get-tuple-element.109, f32[768]{0:T(1024)} %get-tuple-element.106, ...), kind=kLoop, calls=%fused_computation.26 | loop fusion | flops 11403264 | bytes 1594368 | tf_op jit(solution)/shard_map/convert_element_type | solution.py:99
  100.1 2.0 fusion.29
  102.0 2.9 %while.18 = (s32[]{:T(128)}, f32[8,64,128]{2,1,0:T(8,128)S(1)}, f32[2,8,64,128]{3,2,1,0:T(8,128)}, bf16[2,8,64,128]{3,2,1,0:T(8,128)(2,1)}, f32[2,8]{1,0:T(2,128...) while((s32[]{:T(128)}, f32[8,64,128]{2,1,0:T(8,128)S(1)}, ...), condition=%wide.region_7.8_spmd.clone, body=%wide.region_6.7_spmd.clone.sunk | while | flops 196611 | bytes 1310927 | solution.py:147
  104.9 1.7 pad_maximum_fusion.2
  108.6 1.6 compare_and_fusion
  110.2 3.1 %slice.226 = bf16[2048,512]{1,0:T(8,128)(2,1)} slice(bf16[2048,1920]{1,0:T(8,128)(2,1)} %all-gather.4.cloned.1.call-done), slice={[0:2048], [1408:1920]} | slice | bytes 4194304 | tf_op jit(solution)/shard_map/slice | solution.py:74
  113.3 4.3 %reshape.474 = bf16[16,512,128]{2,1,0:T(8,128)(2,1)} reshape(bf16[2048,512]{1,0:T(8,128)(2,1)} %slice.226) | data formatting | bytes 4194304 | tf_op jit(solution)/shard_map/reshape | solution.py:74
  117.6 4.0 %copy.132 = bf16[16,512,128]{1,2,0:T(8,128)(2,1)} copy(bf16[16,512,128]{2,1,0:T(8,128)(2,1)} %reshape.474) | data formatting | bytes 4194304 | tf_op jit(solution)/shard_map/reshape | solution.py:74
  122.5 3.3 %fusion.19 = f32[2,256,8,64]{1,3,2,0:T(8,128)} fusion(f32[2,8,256]{2,1,0:T(8,128)S(1)} %bitcast.108, f32[2,256,256]{2,1,0:T(8,128)S(1)} %fusion.40, f32[2,8,256]{2,1,0:T(8,128)} %copy-done.7, pred[2,256,256]{2,1,0:T(8,128)(4,1)} %compare_and_fusion, bf16[2,256,8,64]{1,0,3,2:T(2,128)(2,1)S(1)} %reshape.467), kind=kOutput, calls=%fused_computation.27 | convolution fusion | flops 140509184 | bytes 2260992 | tf_op jit(solution)/shard_map/chij,cjhp->cihp/dot_general | solution.py:121
  125.9 21.1 %all-gather.6.cloned.1.call-done = bf16[32,8,72,128]{3,2,1,0:T(8,128)(2,1)} async-done(((bf16[2,8,72,128]{3,2,1,0:T(8,128)(2,1)}), bf16[32,8,72,128]{3,2,1,0:T(8,128)(2,1)}) %all-gather.6.cloned.1.call-update) | async-done | bytes 4718608 | tf_op jit(solution)/shard_map/all_gather | solution.py:162
  147.0 1.5 fusion.63
  148.5 5.7 %slice.224 = bf16[16,2,8,64,128]{4,3,2,1,0:T(8,128)(2,1)} slice(bf16[16,2,8,72,128]{4,3,2,1,0:T(8,128)(2,1)} %bitcast.93), slice={[0:16], [0:2], [0:8], [0:64], [0:128]} | slice | bytes 8388608 | tf_op jit(solution)/shard_map/slice | solution.py:163
  155.2 6.3 %fusion.6 = f32[8,1,64,128,1]{3,1,4,2,0:T(1,128)S(1)} fusion(f32[16,2,8,1,1]{0,3,1,4,2:T(1,128)S(1)} %copy.138, bf16[16,2,8,64,128]{4,3,2,1,0:T(8,128)(2,1)} %slice.224), kind=kOutput, calls=%fused_computation.13 | convolution fusion | flops 25165824 | bytes 4457472 | tf_op jit(solution)/shard_map/jch,jchpn->hpn/dot_general | solution.py:179
  164.4 1.6 convolution_convert_fusion
  166.0 1.6 fusion.11
  169.9 5.8 %fusion.22 = f32[2,8,64,128]{3,0,2,1:T(2,128)S(1)} fusion(bf16[16,2,8,64,128]{4,3,2,1,0:T(8,128)(2,1)} %slice.224, f32[2,16,2]{1,0,2:T(2,128)S(1)} %and_convert_fusion, f32[2,16,8]{1,0,2:T(2,128)S(1)} %copy.135, f32[2]{0:T(128)S(1)} %copy-done.23), kind=kOutput, calls=%fused_computation.35 | convolution fusion | flops 50332672 | bytes 4719880 | tf_op jit(solution)/shard_map/rjch,jchpn->rhpn/dot_general | solution.py:220
  176.6 67.9 %reduce-scatter.2.cloned.1.call-done = bf16[64,2176]{1,0:T(8,128)(2,1)} async-done(((bf16[512,2176]{1,0:T(8,128)(2,1)}), bf16[64,2176]{1,0:T(8,128)(2,1)}) %reduce-scatter.2.cloned.1.call-update) | async-done | bytes 278544 | tf_op jit(solution)/shard_map/reduce_scatter | solution.py:200
  (158 shorter events, 31.0 us)
Async XLA Ops:
  7.2 70.0 %copy-start = (bf16[512,2048]{1,0:T(8,128)(2,1)S(1)}, bf16[512,2048]{1,0:T(8,128)(2,1)}, u32[]{:S(2)}) copy-start(bf16[512,2048]{1,0:T(8,128)(2,1)} %param.23) | copy-start | bytes 6291460
  7.2 12.0 %copy-start.6 = (f32[512,128]{1,0:T(8,128)S(1)}, f32[512,128]{1,0:T(8,128)}, u32[]{:S(2)}) copy-start(f32[512,128]{1,0:T(8,128)} %param.35) | copy-start | bytes 786436
  10.3 19.6 %copy-start.25 = (s32[8]{0:T(128)S(1)}, s32[8]{0:T(128)}, u32[]{:S(2)}) copy-start(s32[8]{0:T(128)} %param.36) | copy-start | bytes 100
  10.3 20.4 %copy-start.16 = (f32[512]{0:T(512)S(1)}, f32[512]{0:T(512)}, u32[]{:S(2)}) copy-start(f32[512]{0:T(512)} %param.28) | copy-start | bytes 6148
  10.4 20.4 %copy-start.19 = (f32[256]{0:T(256)S(1)}, f32[256]{0:T(256)}, u32[]{:S(2)}) copy-start(f32[256]{0:T(256)} %param.30) | copy-start | bytes 3076
  10.4 21.0 %copy-start.11 = (f32[4,512]{1,0:T(4,128)S(1)}, f32[4,512]{1,0:T(4,128)}, u32[]{:S(2)}) copy-start(f32[4,512]{1,0:T(4,128)} %param.27) | copy-start | bytes 24580
  10.4 21.0 %copy-start.13 = (f32[4,256]{1,0:T(4,128)S(1)}, f32[4,256]{1,0:T(4,128)}, u32[]{:S(2)}) copy-start(f32[4,256]{1,0:T(4,128)} %param.29) | copy-start | bytes 12292
  10.4 21.8 %copy-start.26 = (f32[8]{0:T(128)S(1)}, f32[8]{0:T(128)}, u32[]{:S(2)}) copy-start(f32[8]{0:T(128)} %param.32) | copy-start | bytes 100
  11.4 17.5 %all-to-all-start = ((bf16[16,8,1408]{2,0,1:T(8,128)(2,1)}), bf16[16,8,1408]{2,0,1:T(8,128)(2,1)S(1)}, u32[]{:S(2)}, u32[]{:S(2)}) async-start(bf16[16,8,1408]{2,0,1:T(8,128)(2,1)} %concatenate.38), calls=%async_computation | async-start | bytes 720896 | tf_op jit(solution)/shard_map/all_to_all | solution.py:66
  19.1 58.0 %all-gather.4.cloned.1.call-start = ((), (), s32[]{:S(2)}) async-start(), calls=%async_computation.2 | async-start | bytes 8355840 | tf_op jit(solution)/shard_map/all_gather | solution.py:70
  29.8 117.1 %all-gather.6.cloned.1.call-start = ((), (), s32[]{:S(2)}) async-start(), calls=%async_computation.4 | async-start | bytes 5013504 | tf_op jit(solution)/shard_map/all_gather | solution.py:162
  30.6 53.6 %copy-start.9 = (s32[2,256]{1,0:T(2,128)}, s32[2,256]{1,0:T(2,128)S(1)}, u32[]{:S(2)}) copy-start(s32[2,256]{1,0:T(2,128)S(1)} %eq.111) | copy-start | bytes 6148
  32.9 51.3 %copy-start.20 = (f32[8]{0:T(128)S(1)}, f32[8]{0:T(128)}, u32[]{:S(2)}) copy-start(f32[8]{0:T(128)} %param.31) | copy-start | bytes 100
  87.6 6.9 %collective-permute-start = (bf16[3,768]{0,1:T(8,128)(2,1)S(1)}, bf16[3,768]{0,1:T(8,128)(2,1)S(1)}, u32[]{:S(2)}, u32[]{:S(2)}) collective-permute-start(bf16[3,768]{0,1:T(8,128)(2,1)S(1)} %slice.203), channel_id=1, source_target_pairs={{0,8},{8,16},{16,24},{24,32},{32,40},{40,48},{48,56},{56,64},{64,7... | collective-permute-start | bytes 13832 | tf_op jit(solution)/shard_map/ppermute | solution.py:14
  106.6 137.8 %reduce-scatter.2.cloned.1.call-start = ((), (), s32[]{:S(2)}) async-start(), calls=%async_computation.3 | async-start | bytes 2506752 | tf_op jit(solution)/shard_map/reduce_scatter | solution.py:200
  117.6 4.6 %copy-start.3 = (bf16[512,128]{0,1:T(8,128)(2,1)S(1)}, bf16[512,128]{0,1:T(8,128)(2,1)}, u32[]{:S(2)}) copy-start(bf16[512,128]{0,1:T(8,128)(2,1)} %get-tuple-element.135) | copy-start | bytes 393220
  148.5 6.1 %copy-start.10 = (pred[16,16]{1,0:T(8,128)(4,1)S(1)}, pred[16,16]{1,0:T(8,128)(4,1)}, u32[]{:S(2)}) copy-start(pred[16,16]{1,0:T(8,128)(4,1)} %broadcast_and_fusion.1) | copy-start | bytes 772
  148.5 6.5 %copy-start.18 = (pred[16]{0:T(512)(128)(4,1)S(1)}, pred[16]{0:T(512)(128)(4,1)}, u32[]{:S(2)}) copy-start(pred[16]{0:T(512)(128)(4,1)} %copy-done.17) | copy-start | bytes 52
  148.5 6.5 %copy-start.23 = (f32[2]{0:T(128)S(1)}, f32[2]{0:T(128)}, u32[]{:S(2)}) copy-start(f32[2]{0:T(128)} %compare_convert_fusion) | copy-start | bytes 28
  155.2 6.3 %copy-start.4 = (f32[2,256,8,64]{1,3,2,0:T(8,128)S(1)}, f32[2,256,8,64]{1,3,2,0:T(8,128)}, u32[]{:S(2)}) copy-start(f32[2,256,8,64]{1,3,2,0:T(8,128)} %fusion.19) | copy-start | bytes 3145732
  155.2 6.3 %copy-start.5 = (f32[2,8,64,128]{3,2,1,0:T(8,128)S(1)}, f32[2,8,64,128]{3,2,1,0:T(8,128)}, u32[]{:S(2)}) copy-start(f32[2,8,64,128]{3,2,1,0:T(8,128)} %get-tuple-element.72) | copy-start | bytes 1572868
  155.2 6.3 %copy-start.8 = (f32[2,256,8]{1,2,0:T(8,128)S(1)}, f32[2,256,8]{1,2,0:T(8,128)}, u32[]{:S(2)}) copy-start(f32[2,256,8]{1,2,0:T(8,128)} %get-tuple-element.129) | copy-start | bytes 49156
  155.2 6.3 %copy-start.12 = (f32[2,8]{1,0:T(2,128)S(1)}, f32[2,8]{1,0:T(2,128)}, u32[]{:S(2)}) copy-start(f32[2,8]{1,0:T(2,128)} %concatenate.43) | copy-start | bytes 196
  155.2 6.3 %copy-start.21 = (f32[8]{0:T(128)S(1)}, f32[8]{0:T(128)}, u32[]{:S(2)}) copy-start(f32[8]{0:T(128)} %param.33) | copy-start | bytes 100
  (9 other events, 17.8 us)
Sparse Core Ops, SparseCore 0:
  29.9 47.1 all-gather.3
  106.8 40.1 all-gather.5
  167.7 76.7 reduce-scatter.1
where the time goes:
time: 254 us; the launch traced here: 253 us
  waiting for transfers between devices  143 us (56%)
  local copies, waits for them, and re-layouts  36 us (14%)
  matrix products  26.6 us (10%)
  other arithmetic  23.1 us (9%)
  between operations  14.3 us (6%)
  starting transfers between devices  9.98 us (4%)
    reduce_scatter x1, waiting for transfers between devices, on_device(): lax.psum_scatter(jnp.concatenate([partial, side], axis=1).astype(jnp.bflo...  67.9 us
    all_gather x1, waiting for transfers between devices, on_device(): lax.all_gather(jnp.concatenate([block, out_piece], axis=1), 'seq', axis=0...  44.3 us
    all_gather x1, waiting for transfers between devices, on_device(): every = lax.all_gather(sendable, 'seq', axis=0, tiled=False)  21.1 us
    all_to_all x1, waiting for transfers between devices, on_device(): lax.all_to_all(packed, 'tp', split_axis=1, concat_axis=0, tiled=True)  9.66 us
    reshape x2, local copies, waits for them, and re-layouts, on_device(): out_block = gathered[:, width:].reshape(seq_count, out_rows, out_cols)  8.31 us
    all_to_all x1, starting transfers between devices, on_device(): lax.all_to_all(packed, 'tp', split_axis=1, concat_axis=0, tiled=True)  7.7 us
    dot_general x1, matrix products, on_device(): proj = jnp.dot(tokens, weights, preferred_element_type=jnp.float32)  7.02 us
    dot_general x1, matrix products, on_device(): jnp.einsum('jch,jchpn->hpn', own_coef, every_end, precision=lax.Precision...  6.27 us
  transfers between devices with their start and end apart: 5, of which 4 were waited for; matrix products, arithmetic and copies ran while one was open for 14% of the time, Pallas kernels for 0%

commit v1 on v0

--- a/solution.py
+++ b/solution.py
@@ -67,8 +67,14 @@
     out_rows, out_cols = w_out.shape
     block_rows = block.shape[0]
     out_piece = w_out.astype(jnp.bfloat16).reshape(block_rows, out_rows * out_cols // block_rows)
-    gathered = lax.all_gather(
-        jnp.concatenate([block, out_piece], axis=1), "seq", axis=0, tiled=True
+    gathered = jnp.concatenate(
+        lax.all_to_all(
+            jnp.stack([jnp.concatenate([block, out_piece], axis=1)] * lax.axis_size("seq")),
+            "seq",
+            0,
+            0,
+        ),
+        axis=0,
     )
     weights = gathered[:, :width]
     out_block = gathered[:, width:].reshape(seq_count, out_rows, out_cols)

time: 254 us -> 337 us (1.33)
  waiting for transfers between devices: 143 us -> 218 us
  starting transfers between devices: 9.98 us -> 14.7 us
  local copies, waits for them, and re-layouts: 36 us -> 40.1 us
    all_to_all x0 -> x1, waiting for transfers between devices: none -> 120 us  [on_device(): lax.all_to_all(jnp.stack([jnp.concatenate([block, out_piece], axis=1)] *...]
    all_gather x1 -> x0, waiting for transfers between devices: 44.3 us -> none  [on_device(): lax.all_gather(jnp.concatenate([block, out_piece], axis=1), 'seq', axis=0...]
    all_to_all x0 -> x1, starting transfers between devices: none -> 5.22 us  [on_device(): lax.all_to_all(jnp.stack([jnp.concatenate([block, out_piece], axis=1)] *...]
    another operation x5 -> x6, local copies, waits for them, and re-layouts: 1.05 us -> 5.26 us  [the longest x1 4.21 us: on_device(): jnp.stack([jnp.concatenate([block, out_piece], axis=1)] * lax.axis_size('...]
    reshape x2 -> x1, local copies, waits for them, and re-layouts: 8.31 us -> 4.35 us  [on_device(): out_block = gathered[:, width:].reshape(seq_count, out_rows, out_cols)]
    transpose x0 -> x1, local copies, waits for them, and re-layouts: none -> 3.96 us  [on_device(): out_block.transpose(1, 0, 2).reshape(out_rows, seq_count * out_cols)]
  transfers between devices with their start and end apart: 5 -> 5, of which waited for: 4 -> 4; matrix products, arithmetic and copies ran while one was open for 14% -> 10% of each run, Pallas kernels for 0% -> 0%
where the time goes in v1:
time: 337 us; the launch traced here: 336 us
  waiting for transfers between devices  218 us (65%)
  local copies, waits for them, and re-layouts  40.1 us (12%)
  matrix products  26.6 us (8%)
  other arithmetic  22.2 us (7%)
  starting transfers between devices  14.7 us (4%)
  between operations  14.5 us (4%)
    all_to_all x1, waiting for transfers between devices, on_device(): lax.all_to_all(jnp.stack([jnp.concatenate([block, out_piece], axis=1)] *...  120 us
    reduce_scatter x1, waiting for transfers between devices, on_device(): lax.psum_scatter(jnp.concatenate([partial, side], axis=1).astype(jnp.bflo...  68 us
    all_gather x1, waiting for transfers between devices, on_device(): every = lax.all_gather(sendable, 'seq', axis=0, tiled=False)  20.4 us
    all_to_all x1, waiting for transfers between devices, on_device(): lax.all_to_all(packed, 'tp', split_axis=1, concat_axis=0, tiled=True)  9.71 us
    all_to_all x1, starting transfers between devices, on_device(): lax.all_to_all(packed, 'tp', split_axis=1, concat_axis=0, tiled=True)  7.7 us
    dot_general x1, matrix products, on_device(): proj = jnp.dot(tokens, weights, preferred_element_type=jnp.float32)  7.03 us
  transfers between devices with their start and end apart: 5, of which 4 were waited for; matrix products, arithmetic and copies ran while one was open for 10% of the time, Pallas kernels for 0%

profile of v1, /device:TPU:0, one launch (start us, length us, event | category | flops | bytes accessed | tf_op | source)
XLA Modules:
  0.0 336.1 jit_solution(1440642024818572375)
XLA Ops:
  11.4 7.7 %all-to-all-start = ((bf16[16,8,1408]{2,0,1:T(8,128)(2,1)}), bf16[16,8,1408]{2,0,1:T(8,128)(2,1)S(1)}, u32[]{:S(2)}, u32[]{:S(2)}) async-start(bf16[16,8,1408]{2,0,1:T(8,128)(2,1)} %concatenate.38), calls=%async_computation | async-start | bytes 720896 | tf_op jit(solution)/shard_map/all_to_all | solution.py:66
  19.2 9.7 %all-to-all-done = bf16[16,8,1408]{2,0,1:T(8,128)(2,1)S(1)} async-done(((bf16[16,8,1408]{2,0,1:T(8,128)(2,1)}), bf16[16,8,1408]{2,0,1:T(8,128)(2,1)S(1)}, u32[]{:S(2)}, u32[]{:S(2)}) %all-to-all-start) | async-done | bytes 360480 | tf_op jit(solution)/shard_map/all_to_all | solution.py:66
  28.9 4.2 %stack.2 = bf16[16,128,1920]{2,1,0:T(8,128)(2,1)} broadcast(bf16[128,1920]{1,0:T(8,128)(2,1)S(1)} %pad_maximum_fusion.1), dimensions={1,2} | broadcast | bytes 8355840 | tf_op jit(solution)/shard_map/stack | solution.py:72
  33.2 5.2 %all-to-all-start.1 = ((bf16[16,128,1920]{2,1,0:T(8,128)(2,1)}), bf16[16,128,1920]{2,1,0:T(8,128)(2,1)}, u32[]{:S(2)}, u32[]{:S(2)}) async-start(bf16[16,128,1920]{2,1,0:T(8,128)(2,1)} %stack.2), calls=%async_computation.1 | async-start | bytes 15728640 | tf_op jit(solution)/shard_map/all_to_all | solution.py:71
  41.5 119.8 %all-to-all-done.1 = bf16[16,128,1920]{2,1,0:T(8,128)(2,1)} async-done(((bf16[16,128,1920]{2,1,0:T(8,128)(2,1)}), bf16[16,128,1920]{2,1,0:T(8,128)(2,1)}, u32[]{:S(2)}, u32[]{:S(2)}) %all-to-all-start.1) | async-done | bytes 7864352 | tf_op jit(solution)/shard_map/all_to_all | solution.py:71
  161.3 7.0 %fusion.65 = (bf16[512,1408]{0,1:T(8,128)(2,1)}, f32[512,1408]{0,1:T(8,128)S(1)}) fusion(bf16[512,2048]{1,0:T(8,128)(2,1)S(1)} %copy-done, bf16[2048,1920]{1,0:T(8,128)(2,1)} %bitcast.6), kind=kOutput, calls=%fused_computation.143 | convolution fusion | flops 2953510912 | bytes 12189696 | tf_op jit(solution)/shard_map/dot_general | solution.py:82
  171.7 1.7 collective-permute-start
  178.2 2.9 multiply_convert_fusion.3
  183.7 2.0 fusion.29
  185.6 2.8 while.18
  188.5 1.7 pad_maximum_fusion.2
  192.1 1.6 compare_and_fusion
  193.7 3.1 slice.226
  196.8 4.3 %reshape.480 = bf16[16,512,128]{2,1,0:T(8,128)(2,1)} reshape(bf16[2048,512]{1,0:T(8,128)(2,1)} %slice.226) | data formatting | bytes 4194304 | tf_op jit(solution)/shard_map/reshape | solution.py:80
  201.1 4.0 %copy.131 = bf16[512,16,128]{0,2,1:T(8,128)(2,1)} copy(bf16[512,16,128]{2,0,1:T(8,128)(2,1)} %bitcast.92) | data formatting | bytes 4194304 | tf_op jit(solution)/shard_map/transpose | solution.py:81
  206.0 3.3 fusion.19
  209.4 20.4 %all-gather.3.cloned.1.call-done = bf16[32,8,72,128]{3,2,1,0:T(8,128)(2,1)} async-done(((bf16[2,8,72,128]{3,2,1,0:T(8,128)(2,1)}), bf16[32,8,72,128]{3,2,1,0:T(8,128)(2,1)}) %all-gather.3.cloned.1.call-update) | async-done | bytes 4718608 | tf_op jit(solution)/shard_map/all_gather | solution.py:168
  229.8 1.5 fusion.63
  231.3 5.7 %slice.224 = bf16[16,2,8,64,128]{4,3,2,1,0:T(8,128)(2,1)} slice(bf16[16,2,8,72,128]{4,3,2,1,0:T(8,128)(2,1)} %bitcast.94), slice={[0:16], [0:2], [0:8], [0:64], [0:128]} | slice | bytes 8388608 | tf_op jit(solution)/shard_map/slice | solution.py:169
  238.0 6.3 %fusion.6 = f32[8,1,64,128,1]{3,1,4,2,0:T(1,128)S(1)} fusion(f32[16,2,8,1,1]{0,3,1,4,2:T(1,128)S(1)} %copy.137, bf16[16,2,8,64,128]{4,3,2,1,0:T(8,128)(2,1)} %slice.224), kind=kOutput, calls=%fused_computation.13 | convolution fusion | flops 25165824 | bytes 4457472 | tf_op jit(solution)/shard_map/jch,jchpn->hpn/dot_general | solution.py:185
  247.3 1.6 convolution_convert_fusion
  248.8 1.6 fusion.11
  252.8 5.8 %fusion.22 = f32[2,8,64,128]{3,0,2,1:T(2,128)S(1)} fusion(bf16[16,2,8,64,128]{4,3,2,1,0:T(8,128)(2,1)} %slice.224, f32[2,16,2]{1,0,2:T(2,128)S(1)} %and_convert_fusion, f32[2,16,8]{1,0,2:T(2,128)S(1)} %copy.134, f32[2]{0:T(128)S(1)} %copy-done.23), kind=kOutput, calls=%fused_computation.35 | convolution fusion | flops 50332672 | bytes 4719880 | tf_op jit(solution)/shard_map/rjch,jchpn->rhpn/dot_general | solution.py:226
  259.4 68.0 %reduce-scatter.2.cloned.1.call-done = bf16[64,2176]{1,0:T(8,128)(2,1)} async-done(((bf16[512,2176]{1,0:T(8,128)(2,1)}), bf16[64,2176]{1,0:T(8,128)(2,1)}) %reduce-scatter.2.cloned.1.call-update) | async-done | bytes 278544 | tf_op jit(solution)/shard_map/reduce_scatter | solution.py:206
  (158 shorter events, 32.6 us)
Async XLA Ops:
  7.2 154.1 %copy-start = (bf16[512,2048]{1,0:T(8,128)(2,1)S(1)}, bf16[512,2048]{1,0:T(8,128)(2,1)}, u32[]{:S(2)}) copy-start(bf16[512,2048]{1,0:T(8,128)(2,1)} %param.23) | copy-start | bytes 6291460
  7.2 11.9 %copy-start.6 = (f32[512,128]{1,0:T(8,128)S(1)}, f32[512,128]{1,0:T(8,128)}, u32[]{:S(2)}) copy-start(f32[512,128]{1,0:T(8,128)} %param.35) | copy-start | bytes 786436
  11.4 17.5 %all-to-all-start = ((bf16[16,8,1408]{2,0,1:T(8,128)(2,1)}), bf16[16,8,1408]{2,0,1:T(8,128)(2,1)S(1)}, u32[]{:S(2)}, u32[]{:S(2)}) async-start(bf16[16,8,1408]{2,0,1:T(8,128)(2,1)} %concatenate.38), calls=%async_computation | async-start | bytes 720896 | tf_op jit(solution)/shard_map/all_to_all | solution.py:66
  33.1 5.3 %copy-start.25 = (s32[8]{0:T(128)S(1)}, s32[8]{0:T(128)}, u32[]{:S(2)}) copy-start(s32[8]{0:T(128)} %param.36) | copy-start | bytes 100
  33.1 6.2 %copy-start.16 = (f32[512]{0:T(512)S(1)}, f32[512]{0:T(512)}, u32[]{:S(2)}) copy-start(f32[512]{0:T(512)} %param.28) | copy-start | bytes 6148
  33.2 6.2 %copy-start.19 = (f32[256]{0:T(256)S(1)}, f32[256]{0:T(256)}, u32[]{:S(2)}) copy-start(f32[256]{0:T(256)} %param.30) | copy-start | bytes 3076
  33.2 6.8 %copy-start.11 = (f32[4,512]{1,0:T(4,128)S(1)}, f32[4,512]{1,0:T(4,128)}, u32[]{:S(2)}) copy-start(f32[4,512]{1,0:T(4,128)} %param.27) | copy-start | bytes 24580
  33.2 6.8 %copy-start.13 = (f32[4,256]{1,0:T(4,128)S(1)}, f32[4,256]{1,0:T(4,128)}, u32[]{:S(2)}) copy-start(f32[4,256]{1,0:T(4,128)} %param.29) | copy-start | bytes 12292
  33.2 7.6 %copy-start.26 = (f32[8]{0:T(128)S(1)}, f32[8]{0:T(128)}, u32[]{:S(2)}) copy-start(f32[8]{0:T(128)} %param.32) | copy-start | bytes 100
  33.2 128.1 %all-to-all-start.1 = ((bf16[16,128,1920]{2,1,0:T(8,128)(2,1)}), bf16[16,128,1920]{2,1,0:T(8,128)(2,1)}, u32[]{:S(2)}, u32[]{:S(2)}) async-start(bf16[16,128,1920]{2,1,0:T(8,128)(2,1)} %stack.2), calls=%async_computation.1 | async-start | bytes 15728640 | tf_op jit(solution)/shard_map/all_to_all | solution.py:71
  38.4 191.4 %all-gather.3.cloned.1.call-start = ((), (), s32[]{:S(2)}) async-start(), calls=%async_computation.4 | async-start | bytes 5013504 | tf_op jit(solution)/shard_map/all_gather | solution.py:168
  39.2 129.1 %copy-start.9 = (s32[2,256]{1,0:T(2,128)}, s32[2,256]{1,0:T(2,128)S(1)}, u32[]{:S(2)}) copy-start(s32[2,256]{1,0:T(2,128)S(1)} %eq.111) | copy-start | bytes 6148
  161.3 7.0 %copy-start.20 = (f32[8]{0:T(128)S(1)}, f32[8]{0:T(128)}, u32[]{:S(2)}) copy-start(f32[8]{0:T(128)} %param.31) | copy-start | bytes 100
  171.7 6.5 %collective-permute-start = (bf16[3,768]{0,1:T(8,128)(2,1)S(1)}, bf16[3,768]{0,1:T(8,128)(2,1)S(1)}, u32[]{:S(2)}, u32[]{:S(2)}) collective-permute-start(bf16[3,768]{0,1:T(8,128)(2,1)S(1)} %slice.203), channel_id=1, source_target_pairs={{0,8},{8,16},{16,24},{24,32},{32,40},{40,48},{48,56},{56,64},{64,7... | collective-permute-start | bytes 13832 | tf_op jit(solution)/shard_map/ppermute | solution.py:14
  190.2 137.2 %reduce-scatter.2.cloned.1.call-start = ((), (), s32[]{:S(2)}) async-start(), calls=%async_computation.3 | async-start | bytes 2506752 | tf_op jit(solution)/shard_map/reduce_scatter | solution.py:206
  201.1 4.6 %copy-start.3 = (bf16[512,128]{0,1:T(8,128)(2,1)S(1)}, bf16[512,128]{0,1:T(8,128)(2,1)}, u32[]{:S(2)}) copy-start(bf16[512,128]{0,1:T(8,128)(2,1)} %get-tuple-element.135) | copy-start | bytes 393220
  231.3 6.1 %copy-start.10 = (pred[16,16]{1,0:T(8,128)(4,1)S(1)}, pred[16,16]{1,0:T(8,128)(4,1)}, u32[]{:S(2)}) copy-start(pred[16,16]{1,0:T(8,128)(4,1)} %broadcast_and_fusion.1) | copy-start | bytes 772
  231.3 6.5 %copy-start.18 = (pred[16]{0:T(512)(128)(4,1)S(1)}, pred[16]{0:T(512)(128)(4,1)}, u32[]{:S(2)}) copy-start(pred[16]{0:T(512)(128)(4,1)} %copy-done.17) | copy-start | bytes 52
  231.3 6.5 %copy-start.23 = (f32[2]{0:T(128)S(1)}, f32[2]{0:T(128)}, u32[]{:S(2)}) copy-start(f32[2]{0:T(128)} %compare_convert_fusion) | copy-start | bytes 28
  238.0 6.3 %copy-start.4 = (f32[2,256,8,64]{1,3,2,0:T(8,128)S(1)}, f32[2,256,8,64]{1,3,2,0:T(8,128)}, u32[]{:S(2)}) copy-start(f32[2,256,8,64]{1,3,2,0:T(8,128)} %fusion.19) | copy-start | bytes 3145732
  238.0 6.3 %copy-start.5 = (f32[2,8,64,128]{3,2,1,0:T(8,128)S(1)}, f32[2,8,64,128]{3,2,1,0:T(8,128)}, u32[]{:S(2)}) copy-start(f32[2,8,64,128]{3,2,1,0:T(8,128)} %get-tuple-element.72) | copy-start | bytes 1572868
  238.0 6.3 %copy-start.8 = (f32[2,256,8]{1,2,0:T(8,128)S(1)}, f32[2,256,8]{1,2,0:T(8,128)}, u32[]{:S(2)}) copy-start(f32[2,256,8]{1,2,0:T(8,128)} %get-tuple-element.129) | copy-start | bytes 49156
  238.0 6.3 %copy-start.12 = (f32[2,8]{1,0:T(2,128)S(1)}, f32[2,8]{1,0:T(2,128)}, u32[]{:S(2)}) copy-start(f32[2,8]{1,0:T(2,128)} %concatenate.43) | copy-start | bytes 196
  238.0 6.3 %copy-start.21 = (f32[8]{0:T(128)S(1)}, f32[8]{0:T(128)}, u32[]{:S(2)}) copy-start(f32[8]{0:T(128)} %param.33) | copy-start | bytes 100
  (9 other events, 15.1 us)
Sparse Core Ops, SparseCore 0:
  190.3 39.4 all-gather.2
  250.5 76.7 reduce-scatter.1
